TPU v7x, 512 devices: a whole 4x4x16 slice. The times are simulated.
512 devices in a mesh: section: 8 (over z_lo), dp: 32 (over x, y, core), tensor: 2 (over z_hi).
Axes of the slice: x: 4, y: 4, z: 16 (z_hi: 2, z_lo: 8; z = z_hi * 8 + z_lo), core: 2. Of those that a mesh axis runs over, the one named last changes fastest.
Arguments:
- hidden_in: bfloat16 [8, 4096, 8192], P('section', ('dp', 'tensor')), may hold values from -600 to 600
- norm_gain: bfloat16 [8, 8192], P('section'), may hold values from 0.5 to 1.5
- value_weight: bfloat16 [8, 8192, 512], P('section', 'dp', 'tensor'), may hold values from -0.0625 to 0.0625
- query_vectors: bfloat16 [8, 4096, 4096], P('section', 'dp', 'tensor'), may hold values from -9 to 9
- key_vectors: bfloat16 [8, 4096, 512], P('section', 'dp', 'tensor'), may hold values from -9 to 9
- grad_attn: bfloat16 [8, 4096, 4096], P('section', 'dp', 'tensor'), may hold values from -250 to 250
- positions: int32 [8, 4096], P('section', 'dp'), may hold values from 0 to 65535, as said below
Outputs:
- value_weight_grad: float32 [8, 8192, 512], P('section', 'dp', 'tensor')
- norm_gain_grad: float32 [8, 8192], P('section')
- to_previous: bfloat16 [8, 4096, 8192], P('section', ('dp', 'tensor'))
Inputs may be any that keep to these rules, and one draw needn't show every extreme that they name: Within each micro-batch of 128 rows, positions rise by one from row to row except at one row between row 32 and row 95, where a new document starts at position 0.
All inputs are finite; a program needn't handle non-finite values.
Results may differ from a plain program's by a relative error of at most 0.014.
Values may be sent and summed in bfloat16 or wider, within the bound.
No kernel may reach another device: no remote copies, remote signals or barrier semaphores. Data moves between devices by JAX's collectives and lax.ppermute only.
A program may use at most 64 MiB of HBM per device.

v0:
```python
import math
import jax
import jax.numpy as jnp
from jax import lax
from jax.sharding import PartitionSpec as P

HD = 128
QPK = 8


def shifted(value, axis, steps):
    count = lax.axis_size(axis)
    first, last = (max(0, -steps), min(count, count - steps))
    return lax.ppermute(value, axis, [(source, source + steps) for source in range(first, last)])


def attend(query_rows, key_rows, grad_rows, position_rows):
    length = query_rows.shape[0]
    groups = key_rows.shape[1] // HD
    query_heads = query_rows.reshape(length, groups, QPK, HD)
    key_heads = key_rows.reshape(length, groups, HD)
    grad_heads = grad_rows.reshape(length, groups, QPK, HD)
    scores = jnp.einsum(
        "igpd,jgd->gpij", query_heads, key_heads, preferred_element_type=jnp.float32
    ) / math.sqrt(HD)
    places = jnp.arange(length, dtype=jnp.int32)
    visible = (places[:, None] >= places[None, :]) & (
        position_rows[:, None] - position_rows[None, :] == places[:, None] - places[None, :]
    )
    masked = jnp.where(visible, scores, jnp.float32(-1e30))
    largest = jnp.max(masked, axis=-1, keepdims=True)
    powers = jnp.where(visible, jnp.exp(masked - largest), jnp.float32(0.0))
    probabilities = powers / jnp.sum(powers, axis=-1, keepdims=True)
    weights = probabilities.astype(jnp.bfloat16)
    value_grad = jnp.einsum(
        "gpij,igpd->jgd", weights, grad_heads, preferred_element_type=jnp.float32
    )
    return value_grad.reshape(length, groups * HD).astype(jnp.bfloat16)


def shards(hidden_in, norm_gain, value_weight, query_vectors, key_vectors, grad_attn, positions):
    rows_float = hidden_in[0].astype(jnp.float32)
    root_mean = jnp.sqrt(jnp.mean(rows_float * rows_float, axis=1, keepdims=True) + 1e-05)
    normed = rows_float / root_mean
    gain_float = norm_gain[0].astype(jnp.float32)
    own_input = (normed * gain_float).astype(jnp.bfloat16)
    layer_input = lax.all_gather(own_input, "tensor", axis=0, tiled=True)
    value_grad = attend(query_vectors[0], key_vectors[0], grad_attn[0], positions[0])
    local_weight = value_weight[0]
    weight_grad = lax.psum_scatter(
        jnp.einsum("tc,tk->ck", layer_input, value_grad, preferred_element_type=jnp.float32).astype(
            jnp.bfloat16
        ),
        "dp",
        scatter_dimension=0,
        tiled=True,
    ).astype(jnp.float32)
    input_part = jnp.einsum(
        "tk,ck->tc",
        value_grad,
        lax.all_gather(local_weight, "dp", axis=0, tiled=True),
        preferred_element_type=jnp.float32,
    ).astype(jnp.bfloat16)
    own_rows = hidden_in.shape[1]
    grad_input = lax.psum(input_part, "tensor").astype(jnp.float32)
    own_grad = lax.dynamic_slice_in_dim(
        grad_input, lax.axis_index("tensor") * own_rows, own_rows, 0
    )
    grad_normed = own_grad * gain_float
    inner_mean = jnp.mean(grad_normed * normed, axis=1, keepdims=True)
    grad_hidden = ((grad_normed - normed * inner_mean) / root_mean).astype(jnp.bfloat16)
    gain_grad = lax.psum(jnp.sum(own_grad * normed, axis=0), ("dp", "tensor"))
    to_previous = shifted(grad_hidden, "section", -1)
    return (weight_grad[None], gain_grad[None], to_previous[None])


def solution(mesh):
    placed = (
        P("section", ("dp", "tensor"), None),
        P("section", None),
        P("section", "dp", "tensor"),
        P("section", "dp", "tensor"),
        P("section", "dp", "tensor"),
        P("section", "dp", "tensor"),
        P("section", "dp"),
    )
    return jax.shard_map(
        shards,
        mesh=mesh,
        in_specs=placed,
        out_specs=(
            P("section", "dp", "tensor"),
            P("section", None),
            P("section", ("dp", "tensor"), None),
        ),
        check_vma=False,
    )
```

profile of v0, /device:TPU:32, one launch (start us, length us, event | category | flops | bytes accessed | tf_op | source)
XLA Modules:
  0.0 1020.2 jit_solution(7451055335804669944)
XLA Ops:
  7.2 0.0 copy-start.3
  7.2 0.0 all-gather.6.cloned.1.call-start
  7.2 0.7 all-gather.6.cloned.1.call-update
  7.9 0.0 all-reduce.2.cloned.1.call-start
  8.0 0.9 reshape_squeeze.9
  8.8 1.1 copy.20
  10.0 1.3 copy.19
  11.3 0.0 copy-done.3
  11.3 0.1 fusion.17
  11.4 0.5 fusion.29
  11.9 0.3 fusion.14
  12.2 64.4 %all-gather.6.cloned.1.call-done = bf16[1,8192,256]{2,1,0:T(8,128)(2,1)} async-done(((bf16[1,256,256]{2,1,0:T(8,128)(2,1)}), bf16[1,8192,256]{2,1,0:T(8,128)(2,1)}) %all-gather.6.cloned.1.call-update) | async-done | bytes 4194320 | tf_op jit(solution)/shard_map/all_gather | solution.py:61
  76.6 5.0 convolution_convert_fusion.1
  81.6 0.0 copy-start.2
  81.6 0.0 copy-start
  81.6 0.0 all-reduce.2.cloned.1.call-update
  81.6 0.0 all-gather.4.cloned.1.call-start
  81.7 0.7 copy-done.2
  82.4 0.4 copy-done
  82.9 0.3 fusion.8
  83.2 215.1 %all-reduce.2.cloned.1.call-done = bf16[128,8192]{1,0:T(8,128)(2,1)} async-done(((bf16[128,8192]{1,0:T(8,128)(2,1)}), bf16[128,8192]{1,0:T(8,128)(2,1)}) %all-reduce.2.cloned.1.call-update) | async-done | bytes 2097168 | tf_op jit(solution)/shard_map/psum | solution.py:65
  298.3 0.0 copy-start.1
  298.3 2.1 fusion.4
  300.4 0.0 copy-done.1
  300.4 1.6 fusion.6
  302.1 0.0 all-gather.4.cloned.1.call-update
  302.1 0.0 reduce-scatter.2.cloned.1.call-start
  302.1 112.5 %all-gather.4.cloned.1.call-done = bf16[128,8192]{1,0:T(8,128)(2,1)} async-done(((bf16[64,8192]{1,0:T(8,128)(2,1)}), bf16[128,8192]{1,0:T(8,128)(2,1)}) %all-gather.4.cloned.1.call-update) | async-done | bytes 2097168 | tf_op jit(solution)/shard_map/all_gather | solution.py:47
  414.6 4.8 convolution_convert_fusion
  419.4 0.0 reduce-scatter.2.cloned.1.call-update
  419.4 15.7 %collective-permute-start = (bf16[64,8192]{1,0:T(8,128)(2,1)S(1)}, bf16[64,8192]{1,0:T(8,128)(2,1)S(1)}, u32[]{:S(2)}, u32[]{:S(2)}) collective-permute-start(bf16[64,8192]{1,0:T(8,128)(2,1)S(1)} %get-tuple-element.5), channel_id=1, source_target_pairs={{64,0},{128,64},{192,128},{256,192},{320,256},{384,320},{448,384},... | collective-permute-start | bytes 3145736 | tf_op jit(solution)/shard_map/ppermute | solution.py:14
  435.2 575.9 %psum.15 = f32[1,8192]{1,0:T(1,128)} all-reduce(f32[1,8192]{1,0:T(1,128)S(1)} %bitcast.58), channel_id=1, replica_groups=mesh['section'=8,'dp'=32,'tensor'=2] {'dp','tensor'}, use_global_device_ids=true, to_apply=%region_6.7 | all-reduce | flops 8192 | bytes 65536 | tf_op jit(solution)/shard_map/psum | solution.py:72
  1011.1 0.0 collective-permute-done
  1011.1 0.0 reduce-scatter.2.cloned.1.call-done
  1011.1 1.6 bitcast_convert_fusion
  1012.7 1.0 copy.39
  (3 shorter events, 0.0 us)
Async XLA Ops:
  7.2 4.1 copy-start.3
  7.2 69.4 %all-gather.6.cloned.1.call-start = ((), (), s32[]{:S(2)}) async-start(), calls=%async_computation.4 | async-start | bytes 4325376 | tf_op jit(solution)/shard_map/all_gather | solution.py:61
  7.9 290.4 %all-reduce.2.cloned.1.call-start = ((), (), s32[]{:S(2)}) async-start(), calls=%async_computation.3 | async-start | bytes 4194304 | tf_op jit(solution)/shard_map/psum | solution.py:65
  81.6 0.8 copy-start.2
  81.6 1.2 copy-start
  81.6 333.0 %all-gather.4.cloned.1.call-start = ((), (), s32[]{:S(2)}) async-start(), calls=%async_computation.1 | async-start | bytes 3145728 | tf_op jit(solution)/shard_map/all_gather | solution.py:47
  298.3 2.1 copy-start.1
  302.1 709.0 %reduce-scatter.2.cloned.1.call-start = ((), (), s32[]{:S(2)}) async-start(), calls=%async_computation.2 | async-start | bytes 4325376 | tf_op jit(solution)/shard_map/reduce_scatter | solution.py:50
  419.4 591.6 %collective-permute-start = (bf16[64,8192]{1,0:T(8,128)(2,1)S(1)}, bf16[64,8192]{1,0:T(8,128)(2,1)S(1)}, u32[]{:S(2)}, u32[]{:S(2)}) collective-permute-start(bf16[64,8192]{1,0:T(8,128)(2,1)S(1)} %get-tuple-element.5), channel_id=1, source_target_pairs={{64,0},{128,64},{192,128},{256,192},{320,256},{384,320},{448,384},... | collective-permute-start | bytes 3145736 | tf_op jit(solution)/shard_map/ppermute | solution.py:14
Sparse Core Ops, SparseCore 0:
  11.1 65.4 all-gather.5
  81.8 216.4 all-reduce.1
  302.2 112.3 all-gather.3
  419.5 110.5 reduce-scatter.1
where the time goes:
time: 1020 us
  blocking collectives  576 us (56%)
  waiting for transfers between devices  393 us (39%)
  starting transfers between devices  15.9 us (2%)
  between operations  13.8 us (1%)
  matrix products  10.7 us (1%)
    psum x1, blocking collectives, shards(): gain_grad = lax.psum(jnp.sum(own_grad * normed, axis=0), ('dp', 'tensor'))  576 us
    psum x1, waiting for transfers between devices, shards(): grad_input = lax.psum(input_part, 'tensor').astype(jnp.float32)  215 us
    all_gather x1, waiting for transfers between devices, shards(): layer_input = lax.all_gather(own_input, 'tensor', axis=0, tiled=True)  112 us
    all_gather x1, waiting for transfers between devices, shards(): lax.all_gather(local_weight, 'dp', axis=0, tiled=True)  64.4 us
  transfers between devices with their start and end apart: 5, of which 3 were waited for; matrix products, arithmetic and copies ran while one was open for 0% of the time, Pallas kernels for 0%

commit v1 on v0

--- a/solution.py
+++ b/solution.py
@@ -69,7 +69,7 @@
     grad_normed = own_grad * gain_float
     inner_mean = jnp.mean(grad_normed * normed, axis=1, keepdims=True)
     grad_hidden = ((grad_normed - normed * inner_mean) / root_mean).astype(jnp.bfloat16)
-    gain_grad = lax.psum(jnp.sum(own_grad * normed, axis=0), ("dp", "tensor"))
+    gain_grad = lax.psum(lax.psum(jnp.sum(own_grad * normed, axis=0), "dp"), "tensor")
     to_previous = shifted(grad_hidden, "section", -1)
     return (weight_grad[None], gain_grad[None], to_previous[None])
 

time: 1020 us -> 589 us (0.58)
  blocking collectives: 576 us -> 144 us
    psum x1 -> x2, blocking collectives: 576 us -> 144 us  [the longest x1 128 us: shards(): lax.psum(jnp.sum(own_grad * normed, axis=0), 'dp')]
  transfers between devices with their start and end apart: 5 -> 5, of which waited for: 3 -> 3; matrix products, arithmetic and copies ran while one was open for 0% -> 1% of each run, Pallas kernels for 0% -> 0%
where the time goes in v1:
time: 589 us
  waiting for transfers between devices  393 us (67%)
  blocking collectives  144 us (24%)
  starting transfers between devices  15.9 us (3%)
  between operations  13.9 us (2%)
  matrix products  10.7 us (2%)
    psum x1, waiting for transfers between devices, shards(): grad_input = lax.psum(input_part, 'tensor').astype(jnp.float32)  215 us
    psum x1, blocking collectives, shards(): lax.psum(jnp.sum(own_grad * normed, axis=0), 'dp')  128 us
    all_gather x1, waiting for transfers between devices, shards(): layer_input = lax.all_gather(own_input, 'tensor', axis=0, tiled=True)  112 us
    all_gather x1, waiting for transfers between devices, shards(): lax.all_gather(local_weight, 'dp', axis=0, tiled=True)  64.4 us
    psum x1, blocking collectives, shards(): lax.psum(lax.psum(jnp.sum(own_grad * normed, axis=0), 'dp'), 'tensor')  16.6 us
    ppermute x1, starting transfers between devices, shifted(): lax.ppermute(value, axis, [(source, source + steps) for source in range(f...  15.7 us
  transfers between devices with their start and end apart: 5, of which 3 were waited for; matrix products, arithmetic and copies ran while one was open for 1% of the time, Pallas kernels for 0%

profile of v1, /device:TPU:32, one launch (start us, length us, event | category | flops | bytes accessed | tf_op | source)
XLA Modules:
  0.0 588.7 jit_solution(18445711897241856517)
XLA Ops:
  7.2 0.0 copy-start.3
  7.2 0.0 all-gather.6.cloned.1.call-start
  7.2 0.7 all-gather.6.cloned.1.call-update
  7.9 0.0 all-reduce.2.cloned.1.call-start
  8.0 0.9 reshape_squeeze.9
  8.8 1.1 copy.20
  10.0 1.3 copy.19
  11.3 0.0 copy-done.3
  11.3 0.1 fusion.17
  11.4 0.5 fusion.29
  11.9 0.3 fusion.14
  12.2 64.4 %all-gather.6.cloned.1.call-done = bf16[1,8192,256]{2,1,0:T(8,128)(2,1)} async-done(((bf16[1,256,256]{2,1,0:T(8,128)(2,1)}), bf16[1,8192,256]{2,1,0:T(8,128)(2,1)}) %all-gather.6.cloned.1.call-update) | async-done | bytes 4194320 | tf_op jit(solution)/shard_map/all_gather | solution.py:61
  76.6 5.0 convolution_convert_fusion.1
  81.6 0.0 copy-start.2
  81.6 0.0 copy-start
  81.6 0.0 all-reduce.2.cloned.1.call-update
  81.6 0.0 all-gather.4.cloned.1.call-start
  81.7 0.7 copy-done.2
  82.4 0.4 copy-done
  82.9 0.3 fusion.8
  83.2 215.1 %all-reduce.2.cloned.1.call-done = bf16[128,8192]{1,0:T(8,128)(2,1)} async-done(((bf16[128,8192]{1,0:T(8,128)(2,1)}), bf16[128,8192]{1,0:T(8,128)(2,1)}) %all-reduce.2.cloned.1.call-update) | async-done | bytes 2097168 | tf_op jit(solution)/shard_map/psum | solution.py:65
  298.3 0.0 copy-start.1
  298.3 2.1 fusion.4
  300.4 0.0 copy-done.1
  300.4 1.6 fusion.6
  302.1 0.0 all-gather.4.cloned.1.call-update
  302.1 0.0 reduce-scatter.2.cloned.1.call-start
  302.1 112.5 %all-gather.4.cloned.1.call-done = bf16[128,8192]{1,0:T(8,128)(2,1)} async-done(((bf16[64,8192]{1,0:T(8,128)(2,1)}), bf16[128,8192]{1,0:T(8,128)(2,1)}) %all-gather.4.cloned.1.call-update) | async-done | bytes 2097168 | tf_op jit(solution)/shard_map/all_gather | solution.py:47
  414.6 4.8 convolution_convert_fusion
  419.4 0.0 reduce-scatter.2.cloned.1.call-update
  419.4 15.7 %collective-permute-start = (bf16[64,8192]{1,0:T(8,128)(2,1)S(1)}, bf16[64,8192]{1,0:T(8,128)(2,1)S(1)}, u32[]{:S(2)}, u32[]{:S(2)}) collective-permute-start(bf16[64,8192]{1,0:T(8,128)(2,1)S(1)} %get-tuple-element.5), channel_id=1, source_target_pairs={{64,0},{128,64},{192,128},{256,192},{320,256},{384,320},{448,384},... | collective-permute-start | bytes 3145736 | tf_op jit(solution)/shard_map/ppermute | solution.py:14
  435.2 127.8 %psum.22 = f32[8192]{0:T(1024)S(1)} all-reduce(f32[8192]{0:T(1024)S(1)} %get-tuple-element.4), channel_id=1, replica_groups=mesh['section'=8,'dp'=32,'tensor'=2] {'dp'}, use_global_device_ids=true, to_apply=%region_6.7 | all-reduce | flops 8192 | bytes 65536 | tf_op jit(solution)/shard_map/psum | solution.py:72
  563.0 16.6 %psum.23 = f32[1,8192]{1,0:T(1,128)} all-reduce(f32[1,8192]{1,0:T(1,128)S(1)} %bitcast.58), channel_id=1, replica_groups=mesh['section'=8,'dp'=32,'tensor'=2] {'tensor'}, use_global_device_ids=true, to_apply=%region_7.8 | all-reduce | flops 8192 | bytes 65536 | tf_op jit(solution)/shard_map/psum | solution.py:72
  579.6 0.0 collective-permute-done
  579.6 0.0 reduce-scatter.2.cloned.1.call-done
  579.6 1.6 bitcast_convert_fusion
  581.2 1.0 copy.39
  (3 shorter events, 0.0 us)
Async XLA Ops:
  7.2 4.1 copy-start.3
  7.2 69.4 %all-gather.6.cloned.1.call-start = ((), (), s32[]{:S(2)}) async-start(), calls=%async_computation.4 | async-start | bytes 4325376 | tf_op jit(solution)/shard_map/all_gather | solution.py:61
  7.9 290.4 %all-reduce.2.cloned.1.call-start = ((), (), s32[]{:S(2)}) async-start(), calls=%async_computation.3 | async-start | bytes 4194304 | tf_op jit(solution)/shard_map/psum | solution.py:65
  81.6 0.8 copy-start.2
  81.6 1.2 copy-start
  81.6 333.0 %all-gather.4.cloned.1.call-start = ((), (), s32[]{:S(2)}) async-start(), calls=%async_computation.1 | async-start | bytes 3145728 | tf_op jit(solution)/shard_map/all_gather | solution.py:47
  298.3 2.1 copy-start.1
  302.1 277.5 %reduce-scatter.2.cloned.1.call-start = ((), (), s32[]{:S(2)}) async-start(), calls=%async_computation.2 | async-start | bytes 4325376 | tf_op jit(solution)/shard_map/reduce_scatter | solution.py:50
  419.4 160.1 %collective-permute-start = (bf16[64,8192]{1,0:T(8,128)(2,1)S(1)}, bf16[64,8192]{1,0:T(8,128)(2,1)S(1)}, u32[]{:S(2)}, u32[]{:S(2)}) collective-permute-start(bf16[64,8192]{1,0:T(8,128)(2,1)S(1)} %get-tuple-element.5), channel_id=1, source_target_pairs={{64,0},{128,64},{192,128},{256,192},{320,256},{384,320},{448,384},... | collective-permute-start | bytes 3145736 | tf_op jit(solution)/shard_map/ppermute | solution.py:14
Sparse Core Ops, SparseCore 0:
  11.1 65.4 all-gather.5
  81.8 216.4 all-reduce.1
  302.2 112.3 all-gather.3
  419.5 110.5 reduce-scatter.1
